TPU v7x, 32 devices: a whole 2x2x4 slice. The times are simulated.
32 devices in a mesh: brick: 8 (over y, x, core), help: 4 (over z).
Axes of the slice: x: 2, y: 2, z: 4, core: 2. Of those that a mesh axis runs over, the one named last changes fastest.
Arguments:
- positions: float32 [3, 2048], P(None, ('brick', 'help')), may hold values from 0 to 1
- velocities: float32 [3, 2048], P(None, ('brick', 'help')), may hold values from -5 to 5
- forces_in: float32 [3, 2048], P(None, ('brick', 'help')), may hold values from -5 to 5
- neighbors: int32 [2048, 128], P(('brick', 'help')), may hold values from -1 to 767, as said below
- w_embed1: float32 [32], replicated, may hold values from -4 to 4
- b_embed1: float32 [32], replicated, may hold values from -3 to 3
- w_embed2: bfloat16 [32, 64], replicated, may hold values from -1 to 1
- b_embed2: float32 [64], replicated, may hold values from -3 to 3
- w_embed3: bfloat16 [64, 128], replicated, may hold values from -0.75 to 0.75
- b_embed3: float32 [128], replicated, may hold values from -3 to 3
- w_fit1: bfloat16 [2048, 240], replicated, may hold values from -0.125 to 0.125
- b_fit1: float32 [240], replicated, may hold values from -3 to 3
- w_fit2: bfloat16 [240, 240], replicated, may hold values from -0.375 to 0.375
- b_fit2: float32 [240], replicated, may hold values from -3 to 3
- w_out: float32 [240], replicated, may hold values from -0.375 to 0.375
Outputs:
- positions_out: float32 [3, 2048], P(None, ('brick', 'help'))
- velocities_out: float32 [3, 2048], P(None, ('brick', 'help'))
- energy: float32 [2048], P(('brick', 'help'))
- forces_out: float32 [3, 2048], P(None, ('brick', 'help'))
Inputs may be any that keep to these rules, and one draw needn't show every extreme that they name: `neighbors`: row i holds atom i's neighbours as table entries: 0 to 255 the atoms of the brick before its own (cyclically), 256 to 511 its own brick, 512 to 767 the brick after; -1 pads. Live entries come first, an entry may repeat, an atom never lists itself. In the first half of the bricks an atom has 96 to 128 live entries, in the other bricks 128 / 4 to 64.
All inputs are finite; a program needn't handle non-finite values.
Results may differ from a plain program's by a relative error of at most 0.011.
Values sent between devices are 32-bit elements; how exact they have to be, the bound alone decides.
No kernel may reach another device: no remote copies, remote signals or barrier semaphores. Data moves between devices by JAX's collectives and lax.ppermute only.
A program may use at most 64 MiB of HBM per device.

v0:
```python
import jax
import jax.numpy as jnp
from jax import lax
from jax.sharding import PartitionSpec as P

NEIGHBOUR_SLOTS = 128
M2 = 16
STEPS = 2
kick_scale = 0.25
time_step = 0.05
highest_precision = lax.Precision.HIGHEST


def extended(value, sides, width):
    for axis, dim in sides:
        size, length = (lax.axis_size(axis), value.shape[dim])
        up = [(i, (i + 1) % size) for i in range(size)]
        down = [(j, i) for i, j in up]
        last = lax.slice_in_dim(value, length - width, length, axis=dim)
        first = lax.slice_in_dim(value, 0, width, axis=dim)
        before = lax.ppermute(last, axis, up)
        after = lax.ppermute(first, axis, down)
        value = jnp.concatenate([before, value, after], axis=dim)
    return value


def pair_terms(displace, live_mask, weights):
    (
        w_embed1,
        b_embed1,
        w_embed2,
        b_embed2,
        w_embed3,
        b_embed3,
        w_fit1,
        b_fit1,
        w_fit2,
        b_fit2,
        w_out,
    ) = weights
    blocks, slot_count = live_mask.shape
    quad_dist = jnp.sum(displace * displace, axis=0) + 0.25
    radius = jnp.sqrt(quad_dist)
    smooth = live_mask / radius
    environment_matrix = jnp.concatenate(
        [smooth[None], live_mask[None] * displace / quad_dist[None]], axis=0
    ).astype(jnp.bfloat16)
    flat_smooth = smooth.reshape(1, -1)
    hidden_first = jnp.tanh(w_embed1[:, None] * flat_smooth + b_embed1[:, None])
    pre_second = (
        jnp.dot(w_embed2.T, hidden_first.astype(jnp.bfloat16), preferred_element_type=jnp.float32)
        + b_embed2[:, None]
    )
    tanh_second = jnp.tanh(pre_second)
    hidden_second = jnp.concatenate([hidden_first, hidden_first], axis=0) + tanh_second
    pre_third = (
        jnp.dot(w_embed3.T, hidden_second.astype(jnp.bfloat16), preferred_element_type=jnp.float32)
        + b_embed3[:, None]
    )
    tanh_third = jnp.tanh(pre_third)
    embedding = (jnp.concatenate([hidden_second, hidden_second], axis=0) + tanh_third).astype(
        jnp.bfloat16
    )
    embedding_width = embedding.shape[0]
    embedding_rows = embedding.reshape(embedding_width, blocks, slot_count)
    descriptor_tensor = (
        jnp.einsum(
            "srj,lrj->rsl", environment_matrix, embedding_rows, preferred_element_type=jnp.float32
        )
        / NEIGHBOUR_SLOTS
    )
    axis_part = descriptor_tensor[:, :, :M2]
    descriptor = jnp.einsum(
        "bce,bck->bek", descriptor_tensor, axis_part, precision=highest_precision
    )
    flat_descr = descriptor.reshape(blocks, -1).astype(jnp.bfloat16)
    fit_hidden = jnp.tanh(jnp.dot(flat_descr, w_fit1, preferred_element_type=jnp.float32) + b_fit1)
    pre_out = (
        jnp.dot(fit_hidden.astype(jnp.bfloat16), w_fit2, preferred_element_type=jnp.float32)
        + b_fit2
    )
    tanh_out = jnp.tanh(pre_out)
    energy = jnp.dot(fit_hidden + tanh_out, w_out, precision=highest_precision)
    grad_out = (w_out[None, :] * (1.0 - tanh_out * tanh_out)).astype(jnp.bfloat16)
    grad_fit = w_out[None, :] + jnp.dot(grad_out, w_fit2.T, preferred_element_type=jnp.float32)
    grad_act = (grad_fit * (1.0 - fit_hidden * fit_hidden)).astype(jnp.bfloat16)
    grad_descr = jnp.dot(grad_act, w_fit1.T, preferred_element_type=jnp.float32).reshape(
        blocks, embedding_width, -1
    )
    grad_tensor = jnp.einsum("bek,bck->bce", grad_descr, axis_part, precision=highest_precision)
    extra_grad = jnp.einsum(
        "bek,bce->bck", grad_descr, descriptor_tensor, precision=highest_precision
    )
    grad_tensor = grad_tensor + jnp.pad(
        extra_grad, ((0, 0), (0, 0), (0, embedding_width - extra_grad.shape[2]))
    )
    descriptor_product_gradient = grad_tensor.astype(jnp.bfloat16)
    environment_gradient = (
        jnp.einsum(
            "ohm,hdo->dhm",
            embedding_rows,
            descriptor_product_gradient,
            preferred_element_type=jnp.float32,
        )
        / NEIGHBOUR_SLOTS
    )
    embedding_gradient = (
        jnp.einsum(
            "zmj,mzr->rmj",
            environment_matrix,
            descriptor_product_gradient,
            preferred_element_type=jnp.float32,
        ).reshape(embedding_width, -1)
        / NEIGHBOUR_SLOTS
    )
    grad_third = (embedding_gradient * (1.0 - tanh_third * tanh_third)).astype(jnp.bfloat16)
    half_width = embedding_width // 2
    grad_hidden2 = (
        embedding_gradient[:half_width]
        + embedding_gradient[half_width:]
        + jnp.dot(w_embed3, grad_third, preferred_element_type=jnp.float32)
    )
    grad_second = (grad_hidden2 * (1.0 - tanh_second * tanh_second)).astype(jnp.bfloat16)
    quarter = half_width // 2
    grad_hidden1 = (
        grad_hidden2[:quarter]
        + grad_hidden2[quarter:]
        + jnp.dot(w_embed2, grad_second, preferred_element_type=jnp.float32)
    )
    grad_smooth = (
        jnp.dot(
            w_embed1,
            grad_hidden1 * (1.0 - hidden_first * hidden_first),
            precision=highest_precision,
        ).reshape(blocks, slot_count)
        + environment_gradient[0]
    )
    radial = jnp.sum(environment_gradient[1:] * displace, axis=0)
    factor = -grad_smooth / (radius * quad_dist) - 2.0 * radial / (quad_dist * quad_dist)
    pair_grad = live_mask[None] * (
        displace * factor[None] + environment_gradient[1:] / quad_dist[None]
    )
    return (energy, pair_grad)


def ghost_table(coords):
    stacked = coords[:, None, :]
    brick_pos = lax.all_gather(stacked, "help", axis=2, tiled=True)
    gathered = extended(brick_pos, (("brick", 1),), 1)
    return gathered.reshape(3, -1)


def return_forces(gathered):
    reduced = lax.psum_scatter(gathered, "help", scatter_dimension=2, tiled=True)
    padded = extended(reduced, (("brick", 1),), 1)
    returned = padded[:, 0] + padded[:, 2] + padded[:, 4]
    return returned


def evaluate(coords, neighbors, weights):
    ghost = ghost_table(coords)
    brick_len = ghost.shape[1] // 3
    atom_count = coords.shape[1]
    safe_index = jnp.maximum(neighbors, 0)
    live_mask = (neighbors >= 0).astype(jnp.float32)
    shift_x = (safe_index // brick_len - 1).astype(jnp.float32)
    block_size = 32
    block_count = atom_count // block_size

    def one_block(pieces):
        own_pos, table_index, offset, mask_rows = pieces
        neighbour_pos = jnp.take(ghost, table_index, axis=1)
        displace = neighbour_pos - own_pos[:, :, None]
        displace = (
            jnp.concatenate([displace[:1] + offset[None], displace[1:]], axis=0) * mask_rows[None]
        )
        return pair_terms(displace, mask_rows, weights)

    own_blocks = coords.reshape(3, block_count, block_size).transpose(1, 0, 2)
    energy, pair_grads = lax.map(
        one_block,
        (
            own_blocks,
            safe_index.reshape(block_count, block_size, -1),
            shift_x.reshape(block_count, block_size, -1),
            live_mask.reshape(block_count, block_size, -1),
        ),
    )
    pair_grads = pair_grads.transpose(1, 0, 2, 3).reshape(3, atom_count, -1)
    energy_rows = energy.reshape(-1)
    gathered = jnp.zeros((3, 3 * brick_len), jnp.float32).at[:, safe_index].add(pair_grads)
    returned = return_forces(gathered.reshape(3, 3, brick_len))
    return (energy_rows, jnp.sum(pair_grads, axis=2) - returned)


def local(
    positions,
    velocities,
    forces_in,
    neighbors,
    w_embed1,
    b_embed1,
    w_embed2,
    b_embed2,
    w_embed3,
    b_embed3,
    w_fit1,
    b_fit1,
    w_fit2,
    b_fit2,
    w_out,
):
    weights = (
        w_embed1,
        b_embed1,
        w_embed2,
        b_embed2,
        w_embed3,
        b_embed3,
        w_fit1,
        b_fit1,
        w_fit2,
        b_fit2,
        w_out,
    )
    coords = positions
    speed = velocities
    force_now = forces_in
    energy = jnp.zeros((positions.shape[1],), jnp.float32)
    for md_step in range(STEPS):
        speed = speed + kick_scale * force_now
        coords = coords + time_step * speed
        energy, force_now = evaluate(coords, neighbors, weights)
        speed = speed + kick_scale * force_now
    return (coords, speed, energy, force_now)


def solution(mesh):
    return jax.shard_map(
        local,
        mesh=mesh,
        in_specs=(
            P(None, ("brick", "help")),
            P(None, ("brick", "help")),
            P(None, ("brick", "help")),
            P(("brick", "help"), None),
            P(),
            P(),
            P(),
            P(),
            P(),
            P(),
            P(),
            P(),
            P(),
            P(),
            P(),
        ),
        out_specs=(
            P(None, ("brick", "help")),
            P(None, ("brick", "help")),
            P(("brick", "help")),
            P(None, ("brick", "help")),
        ),
        check_vma=False,
    )
```

profile of v0, /device:TPU:0, one launch (start us, length us, event | category | flops | bytes accessed | tf_op | source)
XLA Modules:
  0.0 359.1 jit_solution(11644134132301394717)
XLA Ops:
  7.9 13.6 %all-gather.2 = f32[4,64,3]{1,2,0:T(4,128)S(1)} all-gather(f32[1,64,3]{1,2,0:T(4,128)S(1)} %bitcast.479), channel_id=2, replica_groups=mesh['brick'=8,'help'=4] {'help'}, dimensions={0}, use_global_device_ids=true | all-gather | bytes 3840 | tf_op jit(solution)/shard_map/all_gather | solution.py:148
  22.9 1.4 fusion.116
  26.5 71.5 %while.26 = (s32[]{:T(128)}, f32[2,3,32,128]{3,1,2,0:T(4,128)}, f32[2,32,128]{2,0,1:T(2,128)S(1)}, s32[2,32,128]{2,1,0:T(8,128)}, f32[3,768]{0,1:T(8,128)S(1)}, ...) while((s32[]{:T(128)}, f32[2,3,32,128]{3,1,2,0:T(4,128)}, ...), condition=%wide.region_3.5_spmd, body=%wide.region_0.4_spmd.sunk | while | flops 271267840 | bytes 53851500 | solution.py:180
  27.4 10.8 %gather_fusion = f32[4096,3]{1,0:T(8,128)S(1)} fusion(f32[3,768]{0,1:T(8,128)S(1)} %get-tuple-element.963, s32[4096]{0:T(1024)S(1)} %bitcast_clamp_fusion.4), kind=kCustom, calls=%fused_computation.clone.clone.1 | custom fusion | bytes 114688 | tf_op jit(solution)/shard_map/while/body/eval_jaxpr/jit(_take)/gather | solution.py:172
  40.7 2.1 maximum_add_fusion.6
  48.5 1.4 fusion.265
  51.0 1.5 fusion.267
  52.5 1.8 copy.234
  54.3 1.4 fusion.268
  57.8 1.4 fusion.271
  63.1 10.8 %gather_fusion = f32[4096,3]{1,0:T(8,128)S(1)} fusion(f32[3,768]{0,1:T(8,128)S(1)} %get-tuple-element.963, s32[4096]{0:T(1024)S(1)} %bitcast_clamp_fusion.4), kind=kCustom, calls=%fused_computation.clone.clone.1 | custom fusion | bytes 114688 | tf_op jit(solution)/shard_map/while/body/eval_jaxpr/jit(_take)/gather | solution.py:172
  76.5 2.1 maximum_add_fusion.6
  83.0 1.2 copy.233
  84.2 1.4 fusion.265
  86.7 1.5 fusion.267
  88.3 1.8 copy.234
  90.0 1.4 fusion.268
  93.5 1.4 fusion.271
  98.0 3.5 copy.144
  101.6 45.3 %scatter_custom_fusion = f32[3,768]{0,1:T(8,128)S(1)} fusion(s32[8192]{0:T(1024)} %get-tuple-element.670, f32[8192,3]{1,0:T(8,128)} %bitcast.458, f32[]{:T(128)} %constant.160.clone.1), kind=kCustom, calls=%fused_computation.189 | custom fusion | flops 24576 | bytes 9728 | tf_op jit(solution)/shard_map/scatter-add | solution.py:191
  148.1 24.3 %reduce-scatter.7.cloned.1.call-done = f32[64,9]{1,0:T(8,128)} async-done(((f32[256,9]{1,0:T(8,128)}), f32[64,9]{1,0:T(8,128)}) %reduce-scatter.7.cloned.1.call-update) | async-done | bytes 2320
  174.7 2.7 collective-permute-done.2
  178.0 11.9 %all-gather.3 = f32[4,64,3]{1,2,0:T(4,128)S(1)} all-gather(f32[1,64,3]{1,2,0:T(4,128)S(1)} %bitcast.480), channel_id=3, replica_groups=mesh['brick'=8,'help'=4] {'help'}, dimensions={0}, use_global_device_ids=true | all-gather | bytes 3840 | tf_op jit(solution)/shard_map/all_gather | solution.py:148
  191.4 2.8 collective-permute-done.4
  195.8 77.6 %while.27 = (s32[]{:T(128)}, f32[2,32]{1,0:T(2,128)}, f32[2,3,32,128]{3,1,2,0:T(4,128)}, f32[2,32,128]{2,0,1:T(2,128)S(1)}, s32[2,32,128]{2,1,0:T(8,128)}, /*ind...) while((s32[]{:T(128)}, f32[2,32]{1,0:T(2,128)}, ...), condition=%wide.region_10.12_spmd, body=%wide.region_7.11_spmd.sunk | while | flops 271367680 | bytes 45020100 | solution.py:180
  196.6 11.8 %gather_fusion.1 = f32[4096,3]{1,0:T(8,128)S(1)} fusion(f32[3,768]{0,1:T(8,128)} %get-tuple-element.1025, s32[4096]{0:T(1024)S(1)} %bitcast_clamp_fusion.5), kind=kCustom, calls=%fused_computation.1.clone.clone.1 | custom fusion | bytes 114688 | tf_op jit(solution)/shard_map/while/body/eval_jaxpr/jit(_take)/gather | solution.py:172
  211.0 2.1 maximum_add_fusion.7
  218.7 1.4 fusion.304
  221.1 1.3 dynamic_update_slice.27
  222.4 2.4 fusion.307
  224.7 1.7 copy.242
  227.3 1.6 fusion.310
  228.9 1.3 multiply_bitcast_fusion.7
  230.2 1.4 fusion.311
  235.4 11.8 %gather_fusion.1 = f32[4096,3]{1,0:T(8,128)S(1)} fusion(f32[3,768]{0,1:T(8,128)} %get-tuple-element.1025, s32[4096]{0:T(1024)S(1)} %bitcast_clamp_fusion.5), kind=kCustom, calls=%fused_computation.1.clone.clone.1 | custom fusion | bytes 114688 | tf_op jit(solution)/shard_map/while/body/eval_jaxpr/jit(_take)/gather | solution.py:172
  249.7 2.1 maximum_add_fusion.7
  257.4 1.4 fusion.304
  259.9 1.3 dynamic_update_slice.27
  261.1 2.4 fusion.307
  263.5 1.7 copy.242
  266.1 1.6 fusion.310
  267.7 1.3 multiply_bitcast_fusion.7
  269.0 1.4 fusion.311
  273.4 3.5 copy.152
  276.9 45.2 %scatter_custom_fusion.1 = f32[3,768]{0,1:T(8,128)S(1)} fusion(s32[8192]{0:T(1024)} %get-tuple-element.670, f32[8192,3]{1,0:T(8,128)} %bitcast.457, f32[]{:T(128)} %constant.160.clone.1), kind=kCustom, calls=%fused_computation.187 | custom fusion | flops 24576 | bytes 9728 | tf_op jit(solution)/shard_map/scatter-add | solution.py:191
  323.3 23.3 %reduce-scatter.9.cloned.1.call-done = f32[64,9]{1,0:T(8,128)} async-done(((f32[256,9]{1,0:T(8,128)}), f32[64,9]{1,0:T(8,128)}) %reduce-scatter.9.cloned.1.call-update) | async-done | bytes 2320
  348.5 1.3 reshape.307
  349.8 1.8 collective-permute-done.6
  (401 shorter events, 70.9 us)
Async XLA Ops:
  7.2 165.2 %reduce-scatter.7.cloned.1.call-start = ((), (), s32[]{:S(2)}) async-start(), calls=%async_computation.2 | async-start | bytes 163840
  7.9 18.6 %copy-start.58 = (f32[3,64]{1,0:T(4,128)}, f32[3,64]{1,0:T(4,128)S(1)}, u32[]{:S(2)}) copy-start(f32[3,64]{1,0:T(4,128)S(1)} %multiply_add_fusion.2) | copy-start | bytes 2308
  21.6 2.8 collective-permute-start.1
  21.7 4.0 %collective-permute-start = (f32[3,1,256]{2,0,1:T(4,128)S(1)}, f32[3,1,256]{2,0,1:T(4,128)S(1)}, u32[]{:S(2)}, u32[]{:S(2)}) collective-permute-start(f32[3,1,256]{2,0,1:T(4,128)S(1)} %bitcast.482), channel_id=1, source_target_pairs={{0,4},{4,8},{8,12},{12,16},{16,20},{20,24},{24,28},{28,0},{1,5},{5... | collective-permute-start | bytes 9224 | tf_op jit(solution)/shard_map/ppermute | solution.py:21
  26.5 16.3 %copy-start.14 = (f32[3,768]{0,1:T(8,128)}, f32[3,768]{0,1:T(8,128)S(1)}, u32[]{:S(2)}) copy-start(f32[3,768]{0,1:T(8,128)S(1)} %get-tuple-element.963) | copy-start | bytes 27652 | tf_op jit(solution)/shard_map/while
  26.5 16.3 %copy-start.36 = (f32[2,32,128]{2,0,1:T(2,128)}, f32[2,32,128]{2,0,1:T(2,128)S(1)}, u32[]{:S(2)}) copy-start(f32[2,32,128]{2,0,1:T(2,128)S(1)} %get-tuple-element.961) | copy-start | bytes 98308 | tf_op jit(solution)/shard_map/while
  26.5 16.3 %copy-start.40 = (f32[2,32,128]{2,0,1:T(2,128)}, f32[2,32,128]{2,0,1:T(2,128)S(1)}, u32[]{:S(2)}) copy-start(f32[2,32,128]{2,0,1:T(2,128)S(1)} %get-tuple-element.965) | copy-start | bytes 98308 | tf_op jit(solution)/shard_map/while
  26.5 16.3 %copy-start.56 = (f32[2,3,32]{2,1,0:T(4,128)}, f32[2,3,32]{2,1,0:T(4,128)S(1)}, u32[]{:S(2)}) copy-start(f32[2,3,32]{2,1,0:T(4,128)S(1)} %get-tuple-element.964) | copy-start | bytes 2308 | tf_op jit(solution)/shard_map/while
  26.5 14.2 %copy-start.34 = (bf16[32,64]{1,0:T(8,128)(2,1)S(1)}, bf16[32,64]{1,0:T(8,128)(2,1)}, u32[]{:S(2)}) copy-start(bf16[32,64]{1,0:T(8,128)(2,1)} %get-tuple-element.968) | copy-start | bytes 12292 | tf_op jit(solution)/shard_map/while
  44.3 5.6 %copy-start.7 = (bf16[240,240]{1,0:T(8,128)(2,1)S(1)}, bf16[240,240]{1,0:T(8,128)(2,1)}, u32[]{:S(2)}) copy-start(bf16[240,240]{1,0:T(8,128)(2,1)} %get-tuple-element.975) | copy-start | bytes 345604 | tf_op jit(solution)/shard_map/while
  44.3 5.6 %copy-start.50 = (f32[240]{0:T(256)S(1)}, f32[240]{0:T(256)}, u32[]{:S(2)}) copy-start(f32[240]{0:T(256)} %get-tuple-element.976) | copy-start | bytes 2884 | tf_op jit(solution)/shard_map/while
  52.5 4.7 %copy-start.22 = (bf16[3,32,128]{2,0,1:T(4,128)(2,1)S(1)}, bf16[3,32,128]{2,0,1:T(4,128)(2,1)}, u32[]{:S(2)}) copy-start(bf16[3,32,128]{2,0,1:T(4,128)(2,1)} %copy-done.21) | copy-start | bytes 73732 | tf_op jit(solution)/shard_map/while
  52.5 4.7 %copy-start.33 = (bf16[1,32,128]{2,0,1:T(2,128)(2,1)S(1)}, bf16[1,32,128]{2,0,1:T(2,128)(2,1)}, u32[]{:S(2)}) copy-start(bf16[1,32,128]{2,0,1:T(2,128)(2,1)} %copy-done.32) | copy-start | bytes 24580 | tf_op jit(solution)/shard_map/while
  62.3 16.3 %copy-start.14 = (f32[3,768]{0,1:T(8,128)}, f32[3,768]{0,1:T(8,128)S(1)}, u32[]{:S(2)}) copy-start(f32[3,768]{0,1:T(8,128)S(1)} %get-tuple-element.963) | copy-start | bytes 27652 | tf_op jit(solution)/shard_map/while
  62.3 16.3 %copy-start.36 = (f32[2,32,128]{2,0,1:T(2,128)}, f32[2,32,128]{2,0,1:T(2,128)S(1)}, u32[]{:S(2)}) copy-start(f32[2,32,128]{2,0,1:T(2,128)S(1)} %get-tuple-element.961) | copy-start | bytes 98308 | tf_op jit(solution)/shard_map/while
  62.3 16.3 %copy-start.40 = (f32[2,32,128]{2,0,1:T(2,128)}, f32[2,32,128]{2,0,1:T(2,128)S(1)}, u32[]{:S(2)}) copy-start(f32[2,32,128]{2,0,1:T(2,128)S(1)} %get-tuple-element.965) | copy-start | bytes 98308 | tf_op jit(solution)/shard_map/while
  62.3 16.3 %copy-start.56 = (f32[2,3,32]{2,1,0:T(4,128)}, f32[2,3,32]{2,1,0:T(4,128)S(1)}, u32[]{:S(2)}) copy-start(f32[2,3,32]{2,1,0:T(4,128)S(1)} %get-tuple-element.964) | copy-start | bytes 2308 | tf_op jit(solution)/shard_map/while
  62.3 14.2 %copy-start.34 = (bf16[32,64]{1,0:T(8,128)(2,1)S(1)}, bf16[32,64]{1,0:T(8,128)(2,1)}, u32[]{:S(2)}) copy-start(bf16[32,64]{1,0:T(8,128)(2,1)} %get-tuple-element.968) | copy-start | bytes 12292 | tf_op jit(solution)/shard_map/while
  75.5 4.6 %copy-start.18 = (f32[1,32,128]{2,0,1:T(1,128)}, f32[1,32,128]{2,0,1:T(1,128)S(1)}, u32[]{:S(2)}) copy-start(f32[1,32,128]{2,0,1:T(1,128)S(1)} %get-tuple-element.891) | copy-start | bytes 49156 | tf_op jit(solution)/shard_map/while
  80.1 5.6 %copy-start.7 = (bf16[240,240]{1,0:T(8,128)(2,1)S(1)}, bf16[240,240]{1,0:T(8,128)(2,1)}, u32[]{:S(2)}) copy-start(bf16[240,240]{1,0:T(8,128)(2,1)} %get-tuple-element.975) | copy-start | bytes 345604 | tf_op jit(solution)/shard_map/while
  80.1 5.6 %copy-start.50 = (f32[240]{0:T(256)S(1)}, f32[240]{0:T(256)}, u32[]{:S(2)}) copy-start(f32[240]{0:T(256)} %get-tuple-element.976) | copy-start | bytes 2884 | tf_op jit(solution)/shard_map/while
  88.3 4.7 %copy-start.22 = (bf16[3,32,128]{2,0,1:T(4,128)(2,1)S(1)}, bf16[3,32,128]{2,0,1:T(4,128)(2,1)}, u32[]{:S(2)}) copy-start(bf16[3,32,128]{2,0,1:T(4,128)(2,1)} %copy-done.21) | copy-start | bytes 73732 | tf_op jit(solution)/shard_map/while
  88.3 4.7 %copy-start.33 = (bf16[1,32,128]{2,0,1:T(2,128)(2,1)S(1)}, bf16[1,32,128]{2,0,1:T(2,128)(2,1)}, u32[]{:S(2)}) copy-start(bf16[1,32,128]{2,0,1:T(2,128)(2,1)} %copy-done.32) | copy-start | bytes 24580 | tf_op jit(solution)/shard_map/while
  101.5 72.5 %copy-start.49 = (f32[2,3,32,128]{3,1,2,0:T(4,128)S(1)}, f32[2,3,32,128]{3,1,2,0:T(4,128)}, u32[]{:S(2)}) copy-start(f32[2,3,32,128]{3,1,2,0:T(4,128)} %get-tuple-element.460) | copy-start | bytes 294916
  101.5 75.9 %copy-start.59 = (f32[3,64]{1,0:T(4,128)S(1)}, f32[3,64]{1,0:T(4,128)}, u32[]{:S(2)}) copy-start(f32[3,64]{1,0:T(4,128)} %copy-done.58) | copy-start | bytes 2308
  101.5 75.9 %copy-start.62 = (f32[3,64]{1,0:T(4,128)S(1)}, f32[3,64]{1,0:T(4,128)}, u32[]{:S(2)}) copy-start(f32[3,64]{1,0:T(4,128)} %param.22) | copy-start | bytes 2308
  101.5 75.9 %copy-start.63 = (f32[3,64]{1,0:T(4,128)S(1)}, f32[3,64]{1,0:T(4,128)}, u32[]{:S(2)}) copy-start(f32[3,64]{1,0:T(4,128)} %param.23) | copy-start | bytes 2308
  101.5 94.3 %copy-start.1 = (bf16[2048,240]{0,1:T(8,128)(2,1)S(1)}, bf16[2048,240]{0,1:T(8,128)(2,1)}, u32[]{:S(2)}) copy-start(bf16[2048,240]{0,1:T(8,128)(2,1)} %get-tuple-element.1043) | copy-start | bytes 2949124
  101.5 94.3 %copy-start.8 = (bf16[240,240]{1,0:T(8,128)(2,1)S(1)}, bf16[240,240]{1,0:T(8,128)(2,1)}, u32[]{:S(2)}) copy-start(bf16[240,240]{1,0:T(8,128)(2,1)} %get-tuple-element.1044) | copy-start | bytes 345604
  101.5 94.3 %copy-start.35 = (bf16[32,64]{1,0:T(8,128)(2,1)S(1)}, bf16[32,64]{1,0:T(8,128)(2,1)}, u32[]{:S(2)}) copy-start(bf16[32,64]{1,0:T(8,128)(2,1)} %get-tuple-element.1045) | copy-start | bytes 12292
  148.0 198.6 %reduce-scatter.9.cloned.1.call-start = ((), (), s32[]{:S(2)}) async-start(), calls=%async_computation.3 | async-start | bytes 163840
  173.4 1.3 collective-permute-start.3
  173.5 3.9 %collective-permute-start.2 = (f32[3,1,64]{2,0,1:T(4,128)S(1)}, f32[3,1,64]{2,0,1:T(4,128)S(1)}, u32[]{:S(2)}, u32[]{:S(2)}) collective-permute-start(f32[3,1,64]{2,0,1:T(4,128)S(1)} %copy.169), channel_id=1, source_target_pairs={{0,4},{4,8},{8,12},{12,16},{16,20},{20,24},{24,28},{28,0},{1,5},{5... | collective-permute-start | bytes 2312 | tf_op jit(solution)/shard_map/ppermute | solution.py:21
  178.0 17.8 %copy-start.60 = (f32[3,64]{1,0:T(4,128)}, f32[3,64]{1,0:T(4,128)S(1)}, u32[]{:S(2)}) copy-start(f32[3,64]{1,0:T(4,128)S(1)} %get-tuple-element.650) | copy-start | bytes 2308
  190.0 1.3 collective-permute-start.5
  190.0 4.2 %collective-permute-start.4 = (f32[3,1,256]{2,0,1:T(4,128)S(1)}, f32[3,1,256]{2,0,1:T(4,128)S(1)}, u32[]{:S(2)}, u32[]{:S(2)}) collective-permute-start(f32[3,1,256]{2,0,1:T(4,128)S(1)} %bitcast.485), channel_id=1, source_target_pairs={{0,4},{4,8},{8,12},{12,16},{16,20},{20,24},{24,28},{28,0},{1,5},{5... | collective-permute-start | bytes 9224 | tf_op jit(solution)/shard_map/ppermute | solution.py:21
  195.8 13.3 %copy-start.54 = (f32[2,3,32]{2,1,0:T(4,128)}, f32[2,3,32]{2,1,0:T(4,128)S(1)}, u32[]{:S(2)}) copy-start(f32[2,3,32]{2,1,0:T(4,128)S(1)} %get-tuple-element.1026) | copy-start | bytes 2308 | tf_op jit(solution)/shard_map/while
  195.8 17.2 %copy-start.38 = (f32[2,32,128]{2,0,1:T(2,128)}, f32[2,32,128]{2,0,1:T(2,128)S(1)}, u32[]{:S(2)}) copy-start(f32[2,32,128]{2,0,1:T(2,128)S(1)} %get-tuple-element.1023) | copy-start | bytes 98308 | tf_op jit(solution)/shard_map/while
  195.9 17.2 %copy-start.42 = (f32[2,32,128]{2,0,1:T(2,128)}, f32[2,32,128]{2,0,1:T(2,128)S(1)}, u32[]{:S(2)}) copy-start(f32[2,32,128]{2,0,1:T(2,128)S(1)} %get-tuple-element.1027) | copy-start | bytes 98308 | tf_op jit(solution)/shard_map/while
  214.5 5.6 %copy-start.51 = (f32[240]{0:T(256)S(1)}, f32[240]{0:T(256)}, u32[]{:S(2)}) copy-start(f32[240]{0:T(256)} %get-tuple-element.1037) | copy-start | bytes 2884 | tf_op jit(solution)/shard_map/while
  234.6 13.2 %copy-start.54 = (f32[2,3,32]{2,1,0:T(4,128)}, f32[2,3,32]{2,1,0:T(4,128)S(1)}, u32[]{:S(2)}) copy-start(f32[2,3,32]{2,1,0:T(4,128)S(1)} %get-tuple-element.1026) | copy-start | bytes 2308 | tf_op jit(solution)/shard_map/while
  234.6 17.2 %copy-start.38 = (f32[2,32,128]{2,0,1:T(2,128)}, f32[2,32,128]{2,0,1:T(2,128)S(1)}, u32[]{:S(2)}) copy-start(f32[2,32,128]{2,0,1:T(2,128)S(1)} %get-tuple-element.1023) | copy-start | bytes 98308 | tf_op jit(solution)/shard_map/while
  234.7 17.2 %copy-start.42 = (f32[2,32,128]{2,0,1:T(2,128)}, f32[2,32,128]{2,0,1:T(2,128)S(1)}, u32[]{:S(2)}) copy-start(f32[2,32,128]{2,0,1:T(2,128)S(1)} %get-tuple-element.1027) | copy-start | bytes 98308 | tf_op jit(solution)/shard_map/while
  253.3 5.6 %copy-start.51 = (f32[240]{0:T(256)S(1)}, f32[240]{0:T(256)}, u32[]{:S(2)}) copy-start(f32[240]{0:T(256)} %get-tuple-element.1037) | copy-start | bytes 2884 | tf_op jit(solution)/shard_map/while
  276.9 71.3 %copy-start.46 = (f32[2,3,32,128]{3,1,2,0:T(4,128)S(1)}, f32[2,3,32,128]{3,1,2,0:T(4,128)}, u32[]{:S(2)}) copy-start(f32[2,3,32,128]{3,1,2,0:T(4,128)} %get-tuple-element.461) | copy-start | bytes 294916
  276.9 74.7 %copy-start.61 = (f32[3,64]{1,0:T(4,128)S(1)}, f32[3,64]{1,0:T(4,128)}, u32[]{:S(2)}) copy-start(f32[3,64]{1,0:T(4,128)} %get-tuple-element.651) | copy-start | bytes 2308
  347.7 2.2 collective-permute-start.7
  347.7 3.9 %collective-permute-start.6 = (f32[3,1,64]{2,0,1:T(4,128)S(1)}, f32[3,1,64]{2,0,1:T(4,128)S(1)}, u32[]{:S(2)}, u32[]{:S(2)}) collective-permute-start(f32[3,1,64]{2,0,1:T(4,128)S(1)} %copy.172), channel_id=1, source_target_pairs={{0,4},{4,8},{8,12},{12,16},{16,20},{20,24},{24,28},{28,0},{1,5},{5... | collective-permute-start | bytes 2312 | tf_op jit(solution)/shard_map/ppermute | solution.py:21
  (79 other events, 183.6 us)
Sparse Core Ops, SparseCore 0:
  148.2 24.1 reduce-scatter.6
  323.5 23.1 reduce-scatter.8
where the time goes:
time: 362 us; the launch traced here: 359 us
  other arithmetic  107 us (30%)
  local copies, waits for them, and re-layouts  87 us (24%)
  matrix products  64.1 us (18%)
  waiting for transfers between devices  57.3 us (16%)
  blocking collectives  25.5 us (7%)
  between operations  14.2 us (4%)
    scatter-add x2, other arithmetic, evaluate(): jnp.zeros((3, 3 * brick_len), jnp.float32).at[:, safe_index].add(pair_grads)  90.5 us
    unnamed x4, waiting for transfers between devices  47.6 us
    gather x8, local copies, waits for them, and re-layouts, one_block(): neighbour_pos = jnp.take(ghost, table_index, axis=1)  47.5 us
    all_gather x2, blocking collectives, ghost_table(): brick_pos = lax.all_gather(stacked, 'help', axis=2, tiled=True)  25.5 us
    while x212, local copies, waits for them, and re-layouts  8.73 us
    ppermute x4, waiting for transfers between devices, extended(): before = lax.ppermute(last, axis, up)  8.48 us
    dot_general x4, matrix products, pair_terms(): jnp.dot(w_embed2.T, hidden_first.astype(jnp.bfloat16), preferred_element_...  8.38 us
    dot_general x4, matrix products, pair_terms(): jnp.dot(grad_act, w_fit1.T, preferred_element_type=jnp.float32)  7.82 us
  transfers between devices with their start and end apart: 10, of which 8 were waited for; matrix products, arithmetic and copies ran while one was open for 1% of the time, Pallas kernels for 0%

commit v1 on v0

--- a/solution.py
+++ b/solution.py
@@ -145,7 +145,7 @@
 
 def ghost_table(coords):
     stacked = coords[:, None, :]
-    brick_pos = lax.all_gather(stacked, "help", axis=2, tiled=True)
+    brick_pos = jnp.concatenate(lax.all_gather(stacked, "help"), axis=2)
     gathered = extended(brick_pos, (("brick", 1),), 1)
     return gathered.reshape(3, -1)
 

time: 362 us -> 362 us (level)
  no operation moved by 1% of the time
where the time goes in v1:
time: 362 us; the launch traced here: 359 us
  other arithmetic  107 us (30%)
  local copies, waits for them, and re-layouts  87 us (24%)
  matrix products  64.1 us (18%)
  waiting for transfers between devices  57.3 us (16%)
  blocking collectives  25.5 us (7%)
  between operations  14.2 us (4%)
    scatter-add x2, other arithmetic, evaluate(): jnp.zeros((3, 3 * brick_len), jnp.float32).at[:, safe_index].add(pair_grads)  90.5 us
    unnamed x4, waiting for transfers between devices  47.7 us
    gather x8, local copies, waits for them, and re-layouts, one_block(): neighbour_pos = jnp.take(ghost, table_index, axis=1)  47.5 us
    all_gather x2, blocking collectives, ghost_table(): brick_pos = jnp.concatenate(lax.all_gather(stacked, 'help'), axis=2)  25.5 us
    while x212, local copies, waits for them, and re-layouts  8.73 us
    ppermute x4, waiting for transfers between devices, extended(): before = lax.ppermute(last, axis, up)  8.47 us
    dot_general x4, matrix products, pair_terms(): jnp.dot(w_embed2.T, hidden_first.astype(jnp.bfloat16), preferred_element_...  8.38 us
    dot_general x4, matrix products, pair_terms(): jnp.dot(grad_act, w_fit1.T, preferred_element_type=jnp.float32)  7.82 us
  transfers between devices with their start and end apart: 10, of which 8 were waited for; matrix products, arithmetic and copies ran while one was open for 1% of the time, Pallas kernels for 0%

profile of v1, /device:TPU:0, one launch (start us, length us, event | category | flops | bytes accessed | tf_op | source)
XLA Modules:
  0.0 359.1 jit_solution(8350808552154073077)
XLA Ops:
  7.9 13.6 %all-gather.2 = f32[4,3,64]{2,1,0:T(4,128)S(1)} all-gather(f32[1,3,64]{2,1,0:T(4,128)S(1)} %bitcast.473), channel_id=2, replica_groups=mesh['brick'=8,'help'=4] {'help'}, dimensions={0}, use_global_device_ids=true | all-gather | bytes 3840 | tf_op jit(solution)/shard_map/all_gather | solution.py:148
  22.9 1.4 fusion.116
  26.5 71.5 %while.26 = (s32[]{:T(128)}, f32[2,3,32,128]{3,1,2,0:T(4,128)}, f32[2,32,128]{2,0,1:T(2,128)S(1)}, s32[2,32,128]{2,1,0:T(8,128)}, f32[3,768]{0,1:T(8,128)S(1)}, ...) while((s32[]{:T(128)}, f32[2,3,32,128]{3,1,2,0:T(4,128)}, ...), condition=%wide.region_3.5_spmd, body=%wide.region_0.4_spmd.sunk | while | flops 271267840 | bytes 53851500 | solution.py:180
  27.4 10.8 %gather_fusion = f32[4096,3]{1,0:T(8,128)S(1)} fusion(f32[3,768]{0,1:T(8,128)S(1)} %get-tuple-element.926, s32[4096]{0:T(1024)S(1)} %bitcast_clamp_fusion.4), kind=kCustom, calls=%fused_computation.clone.clone.1 | custom fusion | bytes 114688 | tf_op jit(solution)/shard_map/while/body/eval_jaxpr/jit(_take)/gather | solution.py:172
  40.7 2.1 maximum_add_fusion.6
  47.2 1.2 copy.199
  48.5 1.4 fusion.265
  51.0 1.5 fusion.267
  52.5 1.8 copy.200
  54.3 1.4 fusion.268
  57.8 1.4 fusion.271
  63.1 10.8 %gather_fusion = f32[4096,3]{1,0:T(8,128)S(1)} fusion(f32[3,768]{0,1:T(8,128)S(1)} %get-tuple-element.926, s32[4096]{0:T(1024)S(1)} %bitcast_clamp_fusion.4), kind=kCustom, calls=%fused_computation.clone.clone.1 | custom fusion | bytes 114688 | tf_op jit(solution)/shard_map/while/body/eval_jaxpr/jit(_take)/gather | solution.py:172
  76.5 2.1 maximum_add_fusion.6
  84.2 1.4 fusion.265
  86.7 1.5 fusion.267
  88.3 1.8 copy.200
  90.0 1.4 fusion.268
  93.5 1.4 fusion.271
  98.0 3.5 copy.108
  101.6 45.3 %scatter_custom_fusion = f32[3,768]{0,1:T(8,128)S(1)} fusion(s32[8192]{0:T(1024)} %get-tuple-element.633, f32[8192,3]{1,0:T(8,128)} %bitcast.452, f32[]{:T(128)} %constant.160.clone.1), kind=kCustom, calls=%fused_computation.189 | custom fusion | flops 24576 | bytes 9728 | tf_op jit(solution)/shard_map/scatter-add | solution.py:191
  148.1 24.3 %reduce-scatter.7.cloned.1.call-done = f32[64,9]{1,0:T(8,128)} async-done(((f32[256,9]{1,0:T(8,128)}), f32[64,9]{1,0:T(8,128)}) %reduce-scatter.7.cloned.1.call-update) | async-done | bytes 2320
  174.7 2.7 collective-permute-done.2
  178.0 11.9 %all-gather.3 = f32[4,3,64]{2,1,0:T(4,128)S(1)} all-gather(f32[1,3,64]{2,1,0:T(4,128)S(1)} %bitcast.474), channel_id=3, replica_groups=mesh['brick'=8,'help'=4] {'help'}, dimensions={0}, use_global_device_ids=true | all-gather | bytes 3840 | tf_op jit(solution)/shard_map/all_gather | solution.py:148
  191.3 2.8 collective-permute-done.4
  195.8 77.6 %while.27 = (s32[]{:T(128)}, f32[2,32]{1,0:T(2,128)}, f32[2,3,32,128]{3,1,2,0:T(4,128)}, f32[2,32,128]{2,0,1:T(2,128)S(1)}, s32[2,32,128]{2,1,0:T(8,128)}, /*ind...) while((s32[]{:T(128)}, f32[2,32]{1,0:T(2,128)}, ...), condition=%wide.region_10.12_spmd, body=%wide.region_7.11_spmd.sunk | while | flops 271367680 | bytes 45020100 | solution.py:180
  196.6 11.8 %gather_fusion.1 = f32[4096,3]{1,0:T(8,128)S(1)} fusion(f32[3,768]{0,1:T(8,128)} %get-tuple-element.988, s32[4096]{0:T(1024)S(1)} %bitcast_clamp_fusion.5), kind=kCustom, calls=%fused_computation.1.clone.clone.1 | custom fusion | bytes 114688 | tf_op jit(solution)/shard_map/while/body/eval_jaxpr/jit(_take)/gather | solution.py:172
  211.0 2.1 maximum_add_fusion.7
  218.7 1.4 fusion.304
  221.1 1.3 dynamic_update_slice.27
  222.4 2.4 fusion.307
  224.7 1.7 copy.208
  227.3 1.6 fusion.310
  228.9 1.3 multiply_bitcast_fusion.7
  230.2 1.4 fusion.311
  235.4 11.8 %gather_fusion.1 = f32[4096,3]{1,0:T(8,128)S(1)} fusion(f32[3,768]{0,1:T(8,128)} %get-tuple-element.988, s32[4096]{0:T(1024)S(1)} %bitcast_clamp_fusion.5), kind=kCustom, calls=%fused_computation.1.clone.clone.1 | custom fusion | bytes 114688 | tf_op jit(solution)/shard_map/while/body/eval_jaxpr/jit(_take)/gather | solution.py:172
  249.7 2.1 maximum_add_fusion.7
  257.4 1.4 fusion.304
  259.9 1.3 dynamic_update_slice.27
  261.1 2.4 fusion.307
  263.5 1.7 copy.208
  266.1 1.6 fusion.310
  267.7 1.3 multiply_bitcast_fusion.7
  269.0 1.4 fusion.311
  273.4 3.5 copy.116
  276.9 45.2 %scatter_custom_fusion.1 = f32[3,768]{0,1:T(8,128)S(1)} fusion(s32[8192]{0:T(1024)} %get-tuple-element.633, f32[8192,3]{1,0:T(8,128)} %bitcast.451, f32[]{:T(128)} %constant.160.clone.1), kind=kCustom, calls=%fused_computation.187 | custom fusion | flops 24576 | bytes 9728 | tf_op jit(solution)/shard_map/scatter-add | solution.py:191
  323.3 23.3 %reduce-scatter.9.cloned.1.call-done = f32[64,9]{1,0:T(8,128)} async-done(((f32[256,9]{1,0:T(8,128)}), f32[64,9]{1,0:T(8,128)}) %reduce-scatter.9.cloned.1.call-update) | async-done | bytes 2320
  348.5 1.3 reshape.323
  349.8 1.8 collective-permute-done.6
  (401 shorter events, 70.9 us)
Async XLA Ops:
  7.2 165.2 %reduce-scatter.7.cloned.1.call-start = ((), (), s32[]{:S(2)}) async-start(), calls=%async_computation.2 | async-start | bytes 163840
  7.9 18.6 %copy-start.58 = (f32[3,64]{1,0:T(4,128)}, f32[3,64]{1,0:T(4,128)S(1)}, u32[]{:S(2)}) copy-start(f32[3,64]{1,0:T(4,128)S(1)} %multiply_add_fusion.2) | copy-start | bytes 2308
  21.7 2.8 collective-permute-start.1
  21.7 4.0 %collective-permute-start = (f32[3,1,256]{2,1,0:T(1,128)S(1)}, f32[3,1,256]{2,1,0:T(1,128)S(1)}, u32[]{:S(2)}, u32[]{:S(2)}) collective-permute-start(f32[3,1,256]{2,1,0:T(1,128)S(1)} %reshape.311), channel_id=1, source_target_pairs={{0,4},{4,8},{8,12},{12,16},{16,20},{20,24},{24,28},{28,0},{1,5},{5... | collective-permute-start | bytes 9224 | tf_op jit(solution)/shard_map/ppermute | solution.py:21
  26.5 16.3 %copy-start.14 = (f32[3,768]{0,1:T(8,128)}, f32[3,768]{0,1:T(8,128)S(1)}, u32[]{:S(2)}) copy-start(f32[3,768]{0,1:T(8,128)S(1)} %get-tuple-element.926) | copy-start | bytes 27652 | tf_op jit(solution)/shard_map/while
  26.5 16.3 %copy-start.36 = (f32[2,32,128]{2,0,1:T(2,128)}, f32[2,32,128]{2,0,1:T(2,128)S(1)}, u32[]{:S(2)}) copy-start(f32[2,32,128]{2,0,1:T(2,128)S(1)} %get-tuple-element.924) | copy-start | bytes 98308 | tf_op jit(solution)/shard_map/while
  26.5 16.3 %copy-start.40 = (f32[2,32,128]{2,0,1:T(2,128)}, f32[2,32,128]{2,0,1:T(2,128)S(1)}, u32[]{:S(2)}) copy-start(f32[2,32,128]{2,0,1:T(2,128)S(1)} %get-tuple-element.928) | copy-start | bytes 98308 | tf_op jit(solution)/shard_map/while
  26.5 16.3 %copy-start.56 = (f32[2,3,32]{2,1,0:T(4,128)}, f32[2,3,32]{2,1,0:T(4,128)S(1)}, u32[]{:S(2)}) copy-start(f32[2,3,32]{2,1,0:T(4,128)S(1)} %get-tuple-element.927) | copy-start | bytes 2308 | tf_op jit(solution)/shard_map/while
  26.5 14.2 %copy-start.34 = (bf16[32,64]{1,0:T(8,128)(2,1)S(1)}, bf16[32,64]{1,0:T(8,128)(2,1)}, u32[]{:S(2)}) copy-start(bf16[32,64]{1,0:T(8,128)(2,1)} %get-tuple-element.931) | copy-start | bytes 12292 | tf_op jit(solution)/shard_map/while
  44.3 5.6 %copy-start.7 = (bf16[240,240]{1,0:T(8,128)(2,1)S(1)}, bf16[240,240]{1,0:T(8,128)(2,1)}, u32[]{:S(2)}) copy-start(bf16[240,240]{1,0:T(8,128)(2,1)} %get-tuple-element.938) | copy-start | bytes 345604 | tf_op jit(solution)/shard_map/while
  44.3 5.6 %copy-start.50 = (f32[240]{0:T(256)S(1)}, f32[240]{0:T(256)}, u32[]{:S(2)}) copy-start(f32[240]{0:T(256)} %get-tuple-element.939) | copy-start | bytes 2884 | tf_op jit(solution)/shard_map/while
  52.5 4.7 %copy-start.22 = (bf16[3,32,128]{2,0,1:T(4,128)(2,1)S(1)}, bf16[3,32,128]{2,0,1:T(4,128)(2,1)}, u32[]{:S(2)}) copy-start(bf16[3,32,128]{2,0,1:T(4,128)(2,1)} %copy-done.21) | copy-start | bytes 73732 | tf_op jit(solution)/shard_map/while
  52.5 4.7 %copy-start.33 = (bf16[1,32,128]{2,0,1:T(2,128)(2,1)S(1)}, bf16[1,32,128]{2,0,1:T(2,128)(2,1)}, u32[]{:S(2)}) copy-start(bf16[1,32,128]{2,0,1:T(2,128)(2,1)} %copy-done.32) | copy-start | bytes 24580 | tf_op jit(solution)/shard_map/while
  62.3 16.3 %copy-start.14 = (f32[3,768]{0,1:T(8,128)}, f32[3,768]{0,1:T(8,128)S(1)}, u32[]{:S(2)}) copy-start(f32[3,768]{0,1:T(8,128)S(1)} %get-tuple-element.926) | copy-start | bytes 27652 | tf_op jit(solution)/shard_map/while
  62.3 16.3 %copy-start.36 = (f32[2,32,128]{2,0,1:T(2,128)}, f32[2,32,128]{2,0,1:T(2,128)S(1)}, u32[]{:S(2)}) copy-start(f32[2,32,128]{2,0,1:T(2,128)S(1)} %get-tuple-element.924) | copy-start | bytes 98308 | tf_op jit(solution)/shard_map/while
  62.3 16.3 %copy-start.40 = (f32[2,32,128]{2,0,1:T(2,128)}, f32[2,32,128]{2,0,1:T(2,128)S(1)}, u32[]{:S(2)}) copy-start(f32[2,32,128]{2,0,1:T(2,128)S(1)} %get-tuple-element.928) | copy-start | bytes 98308 | tf_op jit(solution)/shard_map/while
  62.3 16.3 %copy-start.56 = (f32[2,3,32]{2,1,0:T(4,128)}, f32[2,3,32]{2,1,0:T(4,128)S(1)}, u32[]{:S(2)}) copy-start(f32[2,3,32]{2,1,0:T(4,128)S(1)} %get-tuple-element.927) | copy-start | bytes 2308 | tf_op jit(solution)/shard_map/while
  62.3 14.2 %copy-start.34 = (bf16[32,64]{1,0:T(8,128)(2,1)S(1)}, bf16[32,64]{1,0:T(8,128)(2,1)}, u32[]{:S(2)}) copy-start(bf16[32,64]{1,0:T(8,128)(2,1)} %get-tuple-element.931) | copy-start | bytes 12292 | tf_op jit(solution)/shard_map/while
  75.5 4.6 %copy-start.18 = (f32[1,32,128]{2,0,1:T(1,128)}, f32[1,32,128]{2,0,1:T(1,128)S(1)}, u32[]{:S(2)}) copy-start(f32[1,32,128]{2,0,1:T(1,128)S(1)} %get-tuple-element.854) | copy-start | bytes 49156 | tf_op jit(solution)/shard_map/while
  80.1 5.6 %copy-start.7 = (bf16[240,240]{1,0:T(8,128)(2,1)S(1)}, bf16[240,240]{1,0:T(8,128)(2,1)}, u32[]{:S(2)}) copy-start(bf16[240,240]{1,0:T(8,128)(2,1)} %get-tuple-element.938) | copy-start | bytes 345604 | tf_op jit(solution)/shard_map/while
  80.1 5.6 %copy-start.50 = (f32[240]{0:T(256)S(1)}, f32[240]{0:T(256)}, u32[]{:S(2)}) copy-start(f32[240]{0:T(256)} %get-tuple-element.939) | copy-start | bytes 2884 | tf_op jit(solution)/shard_map/while
  88.3 4.7 %copy-start.22 = (bf16[3,32,128]{2,0,1:T(4,128)(2,1)S(1)}, bf16[3,32,128]{2,0,1:T(4,128)(2,1)}, u32[]{:S(2)}) copy-start(bf16[3,32,128]{2,0,1:T(4,128)(2,1)} %copy-done.21) | copy-start | bytes 73732 | tf_op jit(solution)/shard_map/while
  88.3 4.7 %copy-start.33 = (bf16[1,32,128]{2,0,1:T(2,128)(2,1)S(1)}, bf16[1,32,128]{2,0,1:T(2,128)(2,1)}, u32[]{:S(2)}) copy-start(bf16[1,32,128]{2,0,1:T(2,128)(2,1)} %copy-done.32) | copy-start | bytes 24580 | tf_op jit(solution)/shard_map/while
  101.5 72.5 %copy-start.49 = (f32[2,3,32,128]{3,1,2,0:T(4,128)S(1)}, f32[2,3,32,128]{3,1,2,0:T(4,128)}, u32[]{:S(2)}) copy-start(f32[2,3,32,128]{3,1,2,0:T(4,128)} %get-tuple-element.460) | copy-start | bytes 294916
  101.5 75.9 %copy-start.59 = (f32[3,64]{1,0:T(4,128)S(1)}, f32[3,64]{1,0:T(4,128)}, u32[]{:S(2)}) copy-start(f32[3,64]{1,0:T(4,128)} %copy-done.58) | copy-start | bytes 2308
  101.5 75.9 %copy-start.62 = (f32[3,64]{1,0:T(4,128)S(1)}, f32[3,64]{1,0:T(4,128)}, u32[]{:S(2)}) copy-start(f32[3,64]{1,0:T(4,128)} %param.22) | copy-start | bytes 2308
  101.5 75.9 %copy-start.63 = (f32[3,64]{1,0:T(4,128)S(1)}, f32[3,64]{1,0:T(4,128)}, u32[]{:S(2)}) copy-start(f32[3,64]{1,0:T(4,128)} %param.23) | copy-start | bytes 2308
  101.5 94.3 %copy-start.1 = (bf16[2048,240]{0,1:T(8,128)(2,1)S(1)}, bf16[2048,240]{0,1:T(8,128)(2,1)}, u32[]{:S(2)}) copy-start(bf16[2048,240]{0,1:T(8,128)(2,1)} %get-tuple-element.1006) | copy-start | bytes 2949124
  101.5 94.3 %copy-start.8 = (bf16[240,240]{1,0:T(8,128)(2,1)S(1)}, bf16[240,240]{1,0:T(8,128)(2,1)}, u32[]{:S(2)}) copy-start(bf16[240,240]{1,0:T(8,128)(2,1)} %get-tuple-element.1007) | copy-start | bytes 345604
  101.5 94.3 %copy-start.35 = (bf16[32,64]{1,0:T(8,128)(2,1)S(1)}, bf16[32,64]{1,0:T(8,128)(2,1)}, u32[]{:S(2)}) copy-start(bf16[32,64]{1,0:T(8,128)(2,1)} %get-tuple-element.1008) | copy-start | bytes 12292
  148.0 198.6 %reduce-scatter.9.cloned.1.call-start = ((), (), s32[]{:S(2)}) async-start(), calls=%async_computation.3 | async-start | bytes 163840
  173.4 1.3 collective-permute-start.3
  173.5 3.9 %collective-permute-start.2 = (f32[3,1,64]{2,0,1:T(4,128)S(1)}, f32[3,1,64]{2,0,1:T(4,128)S(1)}, u32[]{:S(2)}, u32[]{:S(2)}) collective-permute-start(f32[3,1,64]{2,0,1:T(4,128)S(1)} %copy.135), channel_id=1, source_target_pairs={{0,4},{4,8},{8,12},{12,16},{16,20},{20,24},{24,28},{28,0},{1,5},{5... | collective-permute-start | bytes 2312 | tf_op jit(solution)/shard_map/ppermute | solution.py:21
  178.0 17.8 %copy-start.60 = (f32[3,64]{1,0:T(4,128)}, f32[3,64]{1,0:T(4,128)S(1)}, u32[]{:S(2)}) copy-start(f32[3,64]{1,0:T(4,128)S(1)} %get-tuple-element.613) | copy-start | bytes 2308
  190.0 1.3 collective-permute-start.5
  190.0 4.1 %collective-permute-start.4 = (f32[3,1,256]{2,1,0:T(1,128)S(1)}, f32[3,1,256]{2,1,0:T(1,128)S(1)}, u32[]{:S(2)}, u32[]{:S(2)}) collective-permute-start(f32[3,1,256]{2,1,0:T(1,128)S(1)} %reshape.318), channel_id=1, source_target_pairs={{0,4},{4,8},{8,12},{12,16},{16,20},{20,24},{24,28},{28,0},{1,5},{5... | collective-permute-start | bytes 9224 | tf_op jit(solution)/shard_map/ppermute | solution.py:21
  195.8 13.3 %copy-start.54 = (f32[2,3,32]{2,1,0:T(4,128)}, f32[2,3,32]{2,1,0:T(4,128)S(1)}, u32[]{:S(2)}) copy-start(f32[2,3,32]{2,1,0:T(4,128)S(1)} %get-tuple-element.989) | copy-start | bytes 2308 | tf_op jit(solution)/shard_map/while
  195.8 17.2 %copy-start.38 = (f32[2,32,128]{2,0,1:T(2,128)}, f32[2,32,128]{2,0,1:T(2,128)S(1)}, u32[]{:S(2)}) copy-start(f32[2,32,128]{2,0,1:T(2,128)S(1)} %get-tuple-element.986) | copy-start | bytes 98308 | tf_op jit(solution)/shard_map/while
  195.9 17.2 %copy-start.42 = (f32[2,32,128]{2,0,1:T(2,128)}, f32[2,32,128]{2,0,1:T(2,128)S(1)}, u32[]{:S(2)}) copy-start(f32[2,32,128]{2,0,1:T(2,128)S(1)} %get-tuple-element.990) | copy-start | bytes 98308 | tf_op jit(solution)/shard_map/while
  214.5 5.6 %copy-start.51 = (f32[240]{0:T(256)S(1)}, f32[240]{0:T(256)}, u32[]{:S(2)}) copy-start(f32[240]{0:T(256)} %get-tuple-element.1000) | copy-start | bytes 2884 | tf_op jit(solution)/shard_map/while
  234.6 13.2 %copy-start.54 = (f32[2,3,32]{2,1,0:T(4,128)}, f32[2,3,32]{2,1,0:T(4,128)S(1)}, u32[]{:S(2)}) copy-start(f32[2,3,32]{2,1,0:T(4,128)S(1)} %get-tuple-element.989) | copy-start | bytes 2308 | tf_op jit(solution)/shard_map/while
  234.6 17.2 %copy-start.38 = (f32[2,32,128]{2,0,1:T(2,128)}, f32[2,32,128]{2,0,1:T(2,128)S(1)}, u32[]{:S(2)}) copy-start(f32[2,32,128]{2,0,1:T(2,128)S(1)} %get-tuple-element.986) | copy-start | bytes 98308 | tf_op jit(solution)/shard_map/while
  234.6 17.2 %copy-start.42 = (f32[2,32,128]{2,0,1:T(2,128)}, f32[2,32,128]{2,0,1:T(2,128)S(1)}, u32[]{:S(2)}) copy-start(f32[2,32,128]{2,0,1:T(2,128)S(1)} %get-tuple-element.990) | copy-start | bytes 98308 | tf_op jit(solution)/shard_map/while
  253.3 5.6 %copy-start.51 = (f32[240]{0:T(256)S(1)}, f32[240]{0:T(256)}, u32[]{:S(2)}) copy-start(f32[240]{0:T(256)} %get-tuple-element.1000) | copy-start | bytes 2884 | tf_op jit(solution)/shard_map/while
  276.9 71.4 %copy-start.46 = (f32[2,3,32,128]{3,1,2,0:T(4,128)S(1)}, f32[2,3,32,128]{3,1,2,0:T(4,128)}, u32[]{:S(2)}) copy-start(f32[2,3,32,128]{3,1,2,0:T(4,128)} %get-tuple-element.461) | copy-start | bytes 294916
  276.9 74.8 %copy-start.61 = (f32[3,64]{1,0:T(4,128)S(1)}, f32[3,64]{1,0:T(4,128)}, u32[]{:S(2)}) copy-start(f32[3,64]{1,0:T(4,128)} %get-tuple-element.614) | copy-start | bytes 2308
  347.7 2.2 collective-permute-start.7
  347.8 3.9 %collective-permute-start.6 = (f32[3,1,64]{2,0,1:T(4,128)S(1)}, f32[3,1,64]{2,0,1:T(4,128)S(1)}, u32[]{:S(2)}, u32[]{:S(2)}) collective-permute-start(f32[3,1,64]{2,0,1:T(4,128)S(1)} %copy.138), channel_id=1, source_target_pairs={{0,4},{4,8},{8,12},{12,16},{16,20},{20,24},{24,28},{28,0},{1,5},{5... | collective-permute-start | bytes 2312 | tf_op jit(solution)/shard_map/ppermute | solution.py:21
  (79 other events, 183.6 us)
Sparse Core Ops, SparseCore 0:
  148.2 24.1 reduce-scatter.6
  323.4 23.1 reduce-scatter.8
